TPU v7x, 32 devices: a whole 2x2x4 slice. The times are simulated.
32 devices in a mesh: aa: 4 (over x, core), ba: 4 (over z), col: 2 (over y).
Axes of the slice: x: 2, y: 2, z: 4, core: 2. Of those that a mesh axis runs over, the one named last changes fastest.
Arguments:
- tokens: bfloat16 [64, 32, 64, 1024], P('aa', 'ba', 'col'), may hold values from -6 to 6
- norm_gain: float32 [1024], replicated, may hold values from 0.1 to 1.9
- in_weight: bfloat16 [1024, 3072], replicated, may hold values from -0.1875 to 0.1875
- skip_gain: float32 [1024], replicated, may hold values from 0.5 to 1.5
- spectrum_filter: bfloat16 [2, 64, 32, 64, 1024], P(None, ('ba', 'col'), None, None, 'aa'), may hold values from -4 to 4
- out_weight: bfloat16 [1024, 1024], replicated, may hold values from -0.1875 to 0.1875
Outputs:
- layer_out: bfloat16 [64, 32, 64, 1024], P('aa', 'ba', 'col')
All inputs are finite; a program needn't handle non-finite values.
Results may differ from a plain program's by a relative error of at most 0.014.
Values may be sent and summed in bfloat16 or wider, within the bound.
A program may use at most 256 MiB of HBM per device.

v0:
```python
import math

import jax
import jax.numpy as jnp
from jax import lax
from jax.sharding import PartitionSpec as P

LA = 64
LB = 32
LC = 64
D = 1024


EPSILON = 1e-06


def dft_tables(length):
    counter = jnp.arange(length, dtype=jnp.int32)
    product = counter[:, None] * counter[None, :] % length
    angle = 2.0 * math.pi / length * product.astype(jnp.float32)
    factor = 1.0 / math.sqrt(length)
    return (
        (jnp.cos(angle) * factor).astype(jnp.bfloat16),
        (jnp.sin(angle) * factor).astype(jnp.bfloat16),
    )


def phase_pair(integer_phase, modulus):
    angle = 2.0 * math.pi / modulus * (integer_phase % modulus).astype(jnp.float32)
    return (jnp.cos(angle), jnp.sin(angle))


def contract(form, table, operand):
    return jnp.einsum(form, table, operand, preferred_element_type=jnp.float32)


def local(tokens, norm_gain, in_weight, skip_gain, spectrum_filter, out_weight):
    count_aa = lax.axis_size("aa")
    count_ba = lax.axis_size("ba")
    count_col = lax.axis_size("col")
    rows_i = LA // count_aa
    rows_j = LB // count_ba
    rows_k = LC // count_col
    blocks = count_ba * count_col
    freq_local = LA // blocks
    channels = D // count_aa
    points = LA * LB * LC
    flat = tokens.reshape(-1, D).astype(jnp.float32)
    meansq = jnp.mean(flat * flat, axis=-1, keepdims=True)
    normed = (flat * lax.rsqrt(meansq + EPSILON) * norm_gain).astype(jnp.bfloat16)
    projected = jnp.dot(normed, in_weight, preferred_element_type=jnp.float32)
    mixed = (projected[:, :D] * projected[:, 2 * D :]).astype(jnp.bfloat16)
    gate = projected[:, D : 2 * D].astype(jnp.bfloat16)
    local_block = mixed.reshape(rows_i, rows_j, rows_k, D)
    by_rows = lax.all_to_all(local_block, "aa", split_axis=3, concat_axis=0, tiled=True)
    cos_a, sin_a = dft_tables(LA)
    real_part = contract("fi,ijkx->fjkx", cos_a, by_rows)
    imag_part = -contract("fi,ijkx->fjkx", sin_a, by_rows)
    j_global = lax.axis_index("ba") * rows_j + jnp.arange(rows_j, dtype=jnp.int32)
    k_global = lax.axis_index("col") * rows_k + jnp.arange(rows_k, dtype=jnp.int32)
    freq_all = jnp.arange(LA, dtype=jnp.int32)
    cos_phi, sin_phi = phase_pair(
        (LC * j_global[None, :, None] + k_global[None, None, :]) * freq_all[:, None, None], points
    )
    cos_phi = cos_phi[..., None]
    sin_phi = sin_phi[..., None]
    first = jnp.stack(
        [real_part * cos_phi + imag_part * sin_phi, imag_part * cos_phi - real_part * sin_phi]
    ).astype(jnp.bfloat16)
    shaped = first.reshape(2, blocks, 1, freq_local, rows_j, rows_k, channels)
    moved = lax.all_to_all(shaped, ("ba", "col"), split_axis=1, concat_axis=2, tiled=True)
    moved = moved.reshape(2, count_ba, count_col, freq_local, rows_j, rows_k, channels)
    cos_b, sin_b = dft_tables(LB)
    cos_b = cos_b.reshape(LB, count_ba, rows_j)
    sin_b = sin_b.reshape(LB, count_ba, rows_j)
    moved_real = moved[0]
    moved_imag = moved[1]
    form_two = "gbj,bcfjkx->fgckx"
    real_part = contract(form_two, cos_b, moved_real) + contract(form_two, sin_b, moved_imag)
    imag_part = contract(form_two, cos_b, moved_imag) - contract(form_two, sin_b, moved_real)
    index_g = jnp.arange(LB, dtype=jnp.int32)
    index_k = jnp.arange(LC, dtype=jnp.int32)
    cos_psi, sin_psi = phase_pair(index_g[:, None] * index_k[None, :], LB * LC)
    cos_psi = cos_psi.reshape(1, LB, count_col, rows_k, 1)
    sin_psi = sin_psi.reshape(1, LB, count_col, rows_k, 1)
    second_real = (real_part * cos_psi + imag_part * sin_psi).astype(jnp.bfloat16)
    second_imag = (imag_part * cos_psi - real_part * sin_psi).astype(jnp.bfloat16)
    cos_c, sin_c = dft_tables(LC)
    cos_c = cos_c.reshape(LC, count_col, rows_k)
    sin_c = sin_c.reshape(LC, count_col, rows_k)
    form_three = "hck,fgckx->fghx"
    spec_real = contract(form_three, cos_c, second_real) + contract(form_three, sin_c, second_imag)
    spec_imag = contract(form_three, cos_c, second_imag) - contract(form_three, sin_c, second_real)
    filt_real = spectrum_filter[0].astype(jnp.float32)
    filt_imag = spectrum_filter[1].astype(jnp.float32)
    filtered_real = (filt_real * spec_real - filt_imag * spec_imag).astype(jnp.bfloat16)
    filtered_imag = (filt_real * spec_imag + filt_imag * spec_real).astype(jnp.bfloat16)
    form_back_three = "hck,fghx->fgckx"
    real_part = contract(form_back_three, cos_c, filtered_real) - contract(
        form_back_three, sin_c, filtered_imag
    )
    imag_part = contract(form_back_three, cos_c, filtered_imag) + contract(
        form_back_three, sin_c, filtered_real
    )
    third_real = (real_part * cos_psi - imag_part * sin_psi).astype(jnp.bfloat16)
    third_imag = (imag_part * cos_psi + real_part * sin_psi).astype(jnp.bfloat16)
    form_back_two = "gbj,fgckx->bcfjkx"
    real_part = contract(form_back_two, cos_b, third_real) - contract(
        form_back_two, sin_b, third_imag
    )
    imag_part = contract(form_back_two, cos_b, third_imag) + contract(
        form_back_two, sin_b, third_real
    )
    slot = lax.axis_index("ba") * count_col + lax.axis_index("col")
    freq_global = slot * freq_local + jnp.arange(freq_local, dtype=jnp.int32)
    j_all = jnp.arange(LB, dtype=jnp.int32).reshape(count_ba, rows_j)
    k_all = jnp.arange(LC, dtype=jnp.int32).reshape(count_col, rows_k)
    integer_phase = (
        LC * j_all[:, None, None, :, None] + k_all[None, :, None, None, :]
    ) * freq_global[None, None, :, None, None]
    cos_back, sin_back = phase_pair(integer_phase, points)
    cos_back = cos_back[..., None]
    sin_back = sin_back[..., None]
    back_second = jnp.stack(
        [real_part * cos_back - imag_part * sin_back, imag_part * cos_back + real_part * sin_back]
    ).astype(jnp.bfloat16)
    shaped = back_second.reshape(2, 1, blocks, freq_local, rows_j, rows_k, channels)
    returned = lax.all_to_all(shaped, ("ba", "col"), split_axis=2, concat_axis=1, tiled=True)
    returned = returned.reshape(2, LA, rows_j, rows_k, channels)
    conv_part = (
        contract("fi,fjkx->ijkx", cos_a, returned[0])
        - contract("fi,fjkx->ijkx", sin_a, returned[1])
    ).astype(jnp.bfloat16)
    conv_tokens = lax.all_to_all(conv_part, "aa", split_axis=0, concat_axis=3, tiled=True)
    conv_flat = conv_tokens.reshape(-1, D).astype(jnp.float32)
    gated = (gate.astype(jnp.float32) * (conv_flat + skip_gain * mixed.astype(jnp.float32))).astype(
        jnp.bfloat16
    )
    layer_out = jnp.dot(gated, out_weight, preferred_element_type=jnp.float32).astype(jnp.bfloat16)
    return layer_out.reshape(rows_i, rows_j, rows_k, D)


def solution(mesh):
    in_specs = (
        P("aa", "ba", "col", None),
        P(),
        P(),
        P(),
        P(None, ("ba", "col"), None, None, "aa"),
        P(),
    )
    out_specs = P("aa", "ba", "col", None)
    return jax.shard_map(local, mesh=mesh, in_specs=in_specs, out_specs=out_specs, check_vma=False)
```

profile of v0, /device:TPU:0, one launch (start us, length us, event | category | flops | bytes accessed | tf_op | source)
XLA Modules:
  0.0 1626.5 jit_solution(17985871560991421885)
XLA Ops:
  0.0 5.2 multiply_reduce_fusion
  5.4 5.4 fusion.14
  10.8 31.4 %fusion.236 = f32[4096,3072]{1,0:T(8,128)} fusion(bf16[4096,1024]{1,0:T(8,128)(2,1)S(1)} %fusion.14, bf16[1024,3072]{1,0:T(8,128)(2,1)S(1)} %copy-done.8), kind=kOutput, calls=%fused_computation.280 | convolution fusion | flops 25769803776 | bytes 65011712 | tf_op jit(solution)/shard_map/dot_general | solution.py:51
  42.2 15.1 fusion.4
  57.4 44.2 %copy.74 = bf16[16,8,32,1024]{2,1,0,3:T(8,128)(2,1)} copy(bf16[16,8,32,1024]{3,2,1,0:T(8,128)(2,1)} %bitcast.244) | data formatting | bytes 16777216 | tf_op jit(solution)/shard_map/reshape | solution.py:54
  101.6 50.4 %reshape.452 = bf16[4,2,524288]{2,1,0:T(2,128)(2,1)} reshape(bf16[1024,16,8,32]{3,2,1,0:T(8,128)(2,1)} %bitcast.236) | data formatting | bytes 16777216
  152.0 6.1 all-to-all-start
  159.5 92.4 %all-to-all-done = bf16[4,2,524288]{2,1,0:T(2,128)(2,1)} async-done(((bf16[4,2,524288]{2,1,0:T(2,128)(2,1)}), bf16[4,2,524288]{2,1,0:T(2,128)(2,1)}, u32[]{:S(2)}, u32[]{:S(2)}) %all-to-all-start) | async-done | bytes 8388640 | tf_op jit(solution)/shard_map/all_to_all | solution.py:55
  251.9 37.0 %reshape.453 = bf16[1024,16,8,32]{3,2,1,0:T(8,128)(2,1)} reshape(bf16[4,2,524288]{2,1,0:T(2,128)(2,1)} %all-to-all-done) | data formatting | bytes 16777216
  288.9 45.4 %copy.75 = bf16[16,8,32,4,256]{4,0,3,2,1:T(8,128)(2,1)} copy(bf16[16,8,32,4,256]{2,1,0,4,3:T(8,128)(2,1)} %bitcast.235) | data formatting | bytes 16777216 | tf_op jit(solution)/shard_map/all_to_all | solution.py:55
  334.3 6.0 fusion.107
  340.3 11.3 fusion.15
  351.6 11.4 copy.78
  363.0 11.4 copy.79
  374.4 13.8 pad_maximum_fusion
  388.2 6.6 all-to-all-start.1
  397.7 1.4 copy.97
  399.1 358.3 %all-to-all-done.1 = bf16[2,8,1,8,8,32,256]{6,5,4,3,2,0,1:T(8,128)(2,1)} async-done(((bf16[2,8,1,8,8,32,256]{6,5,4,3,2,0,1:T(8,128)(2,1)}), bf16[2,8,1,8,8,32,256]{6,5,4,3,2,0,1:T(8,128)(2,1)}, u32[]{:S(2)}, u32[]{:S(2)}) %all-to-all-start.1) | async-done | bytes 16777248 | tf_op jit(solution)/shard_map/all_to_all | solution.py:71
  757.4 10.3 fusion.227
  767.8 17.5 %fusion.45 = f32[2,8,32,256,32,1]{3,4,5,2,1,0:T(8,128)} fusion(bf16[4,2,8,8,32,256]{5,4,3,2,1,0:T(8,128)(2,1)} %bitcast.241, s32[4,8]{1,0:T(4,128)S(1)} %multiply_add_fusion), kind=kOutput, calls=%fused_computation.77 | convolution fusion | flops 268451840 | bytes 25165952 | tf_op jit(solution)/shard_map/gbj,bcfjkx->fgckx/dot_general | solution.py:34
  785.3 14.3 fusion.47
  799.6 8.9 fusion.41
  808.5 26.6 %fusion.10 = (bf16[8,32,2,32,256]{4,1,3,0,2:T(8,128)(2,1)}, bf16[8,32,2,32,256]{4,1,3,0,2:T(8,128)(2,1)}) fusion(f32[32,2,32]{0,2,1:T(8,128)S(1)} %get-tuple-element.24, f32[32,2,32]{0,2,1:T(8,128)S(1)} %get-tuple-element.23, f32[2,8,32,256,32,1]{3,4,5,2,1,0:T(8,128)} %fusion.47, f32[2,8,32,256,32,1]{3,4,5,2,1,0:T(8,128)} %fusion.45, ...), kind=kOutput, calls=%fused_computation.26 | convolution fusion | flops 310394880 | bytes 75513984 | tf_op jit(solution)/shard_map/gbj,bcfjkx->fgckx/dot_general | solution.py:34
  835.2 16.0 fusion.35
  851.2 12.4 fusion.39
  863.5 21.3 %bitcast_subtract_fusion = f32[8,32,256,64]{2,3,1,0:T(8,128)} fusion(f32[8,32,256,64,1]{2,3,4,1,0:T(8,128)} %fusion.35, bf16[8,32,2,32,256]{4,1,3,0,2:T(8,128)(2,1)} %get-tuple-element.5, s32[2,32]{1,0:T(2,128)S(1)} %multiply_add_fusion.1), kind=kOutput, calls=%fused_computation.21 | convolution fusion | flops 541130752 | bytes 41943296 | tf_op jit(solution)/shard_map/hck,fgckx->fghx/dot_general | solution.py:34
  884.8 24.5 %fusion.20 = (bf16[8,32,64,256,1]{3,2,4,1,0:T(8,128)(2,1)}, bf16[8,32,64,256,1]{3,2,4,1,0:T(8,128)(2,1)S(1)}) fusion(f32[8,32,256,64]{2,3,1,0:T(8,128)} %bitcast_subtract_fusion, bf16[2,8,32,64,256]{4,3,2,1,0:T(8,128)(2,1)} %param.10, s32[2,32]{1,0:T(2,128)S(1)} %multiply_add_fusion.1, bf16[8,32,2,32,256]{4,1,3,0,2:T(8,128)(2,1)} %get-tuple-element.6, ...), kind=kOutput, calls=%fused_computation.52 | convolution fusion | flops 583073792 | bytes 75497728 | tf_op jit(solution)/shard_map/hck,fgckx->fghx/dot_general | solution.py:34
  909.3 11.7 fusion.96
  921.0 8.2 fusion.98
  929.2 14.1 convolution_add_fusion.1
  943.3 19.4 %fusion.17 = (bf16[8,32,2,32,256,1]{4,3,2,1,0,5:T(8,128)(2,1)S(1)}, bf16[8,32,2,32,256,1]{4,3,2,1,0,5:T(8,128)(2,1)}) fusion(f32[8,32,256,2,32]{2,4,3,1,0:T(8,128)} %convolution_add_fusion.1, f32[32,2,32]{2,1,0:T(2,128)S(1)} %copy.91, f32[32,2,32]{2,1,0:T(2,128)S(1)} %copy.90, f32[8,32,256,2,32]{2,4,3,1,0:T(8,128)} %fusion.98, ...), kind=kOutput, calls=%fused_computation.49 | convolution fusion | flops 574685184 | bytes 58736896 | tf_op jit(solution)/shard_map/hck,fghx->fgckx/dot_general | solution.py:34
  962.6 11.0 fusion.33
  973.7 14.3 fusion.29
  988.0 20.0 %convolution_subtract_fusion = f32[8,2,32,256,4,8]{3,5,4,2,1,0:T(8,128)} fusion(f32[8,2,32,256,4,8]{3,5,4,2,1,0:T(8,128)} %fusion.33, bf16[8,32,2,32,256,1]{4,3,2,1,0,5:T(8,128)(2,1)} %get-tuple-element.14, s32[4,8]{1,0:T(4,128)S(1)} %multiply_add_fusion), kind=kOutput, calls=%fused_computation.44 | convolution fusion | flops 272646144 | bytes 41943168 | tf_op jit(solution)/shard_map/gbj,fgckx->bcfjkx/dot_general | solution.py:34
  1008.0 23.1 %fusion.6 = (bf16[4,2,8,8,32,256]{5,3,0,4,1,2:T(8,128)(2,1)}, bf16[4,2,8,8,32,256]{5,3,0,4,1,2:T(8,128)(2,1)}) fusion(f32[8,2,32,256,4,8]{3,5,4,2,1,0:T(8,128)} %convolution_subtract_fusion, f32[4,2,8,8,32]{3,0,4,1,2:T(4,128)S(1)} %copy-done.6, f32[4,2,8,8,32]{3,0,4,1,2:T(4,128)S(1)} %copy-done.5, f32[8,2,32,256,4,8]{3,5,4,2,1,0:T(8,128)} %fusion.29, ...), kind=kOutput, calls=%fused_computation.16 | convolution fusion | flops 306200576 | bytes 58851456 | tf_op jit(solution)/shard_map/gbj,fgckx->bcfjkx/dot_general | solution.py:34
  1031.1 15.7 copy.98
  1046.9 15.9 copy.99
  1062.8 8.0 pad_maximum_fusion.1
  1070.8 6.8 copy.100
  1077.5 367.5 %all_to_all.45 = bf16[2,1,8,8,8,32,256]{6,5,4,3,1,0,2:T(8,128)(2,1)S(1)} all-to-all(bf16[2,1,8,8,8,32,256]{6,5,4,3,1,0,2:T(8,128)(2,1)} %copy.100), channel_id=1, replica_groups=mesh['aa'=4,'ba'=4,'col'=2] {'ba','col'}, dimensions={2} | all-to-all | bytes 33554432 | tf_op jit(solution)/shard_map/all_to_all | solution.py:128
  1445.1 5.0 fusion.226
  1450.0 12.5 fusion.23
  1462.5 21.2 %subtract_convert_fusion = bf16[64,8,32,256]{3,0,2,1:T(8,128)(2,1)} fusion(f32[64,8,32,256]{3,0,2,1:T(8,128)} %fusion.23, bf16[1,1,8,8,8,32,256]{6,5,4,3,1,0,2:T(8,128)(2,1)} %get-tuple-element.15), kind=kOutput, calls=%fused_computation.37 | convolution fusion | flops 545325056 | bytes 33554432 | tf_op jit(solution)/shard_map/fi,fjkx->ijkx/dot_general | solution.py:34
  1483.7 11.4 copy.103
  1495.1 97.2 %all_to_all.46 = bf16[64,8,32,256]{3,2,1,0:T(8,128)(2,1)S(1)} all-to-all(bf16[64,8,32,256]{3,2,1,0:T(8,128)(2,1)} %copy.103), channel_id=1, replica_groups=mesh['aa'=4,'ba'=4,'col'=2] {'aa'}, dimensions={0} | all-to-all | bytes 16777216 | tf_op jit(solution)/shard_map/all_to_all | solution.py:134
  1592.3 6.9 copy.104
  1599.2 8.2 copy.141
  1607.4 18.7 %fusion.28 = bf16[4096,1024]{1,0:T(8,128)(2,1)} fusion(bf16[1024,1024]{1,0:T(8,128)(2,1)S(1)} %copy-done, f32[4096,1024]{1,0:T(8,128)} %bitcast.250, bf16[4096,1024]{1,0:T(8,128)(2,1)S(1)} %bitcast.246, f32[4096,3072]{1,0:T(8,128)} %fusion.236, f32[1024]{0:T(1024)S(1)} %copy-done.9), kind=kOutput, calls=%fused_computation.60 | convolution fusion | flops 8619294720 | bytes 44044288 | tf_op jit(solution)/shard_map/dot_general | solution.py:139
  (41 shorter events, 4.4 us)
Async XLA Ops:
  0.0 1607.3 %copy-start = (bf16[1024,1024]{1,0:T(8,128)(2,1)S(1)}, bf16[1024,1024]{1,0:T(8,128)(2,1)}, u32[]{:S(2)}) copy-start(bf16[1024,1024]{1,0:T(8,128)(2,1)} %param.11) | copy-start | bytes 6291460
  0.0 5.4 copy-start.7
  5.4 5.4 copy-start.8
  152.0 99.9 %all-to-all-start = ((bf16[4,2,524288]{2,1,0:T(2,128)(2,1)}), bf16[4,2,524288]{2,1,0:T(2,128)(2,1)}, u32[]{:S(2)}, u32[]{:S(2)}) async-start(bf16[4,2,524288]{2,1,0:T(2,128)(2,1)} %reshape.452), calls=%async_computation | async-start | bytes 16777216 | tf_op jit(solution)/shard_map/all_to_all | solution.py:55
  334.3 6.0 copy-start.3
  388.2 369.3 %all-to-all-start.1 = ((bf16[2,8,1,8,8,32,256]{6,5,4,3,2,0,1:T(8,128)(2,1)}), bf16[2,8,1,8,8,32,256]{6,5,4,3,2,0,1:T(8,128)(2,1)}, u32[]{:S(2)}, u32[]{:S(2)}) async-start(bf16[2,8,1,8,8,32,256]{6,5,4,3,2,0,1:T(8,128)(2,1)} %pad_maximum_fusion), calls=%async_computation.1 | async-start | bytes 33554432 | tf_op jit(solution)/shard_map/all_to_all | solution.py:71
  767.8 31.8 %copy-start.4 = (bf16[1,8,1,8,8,32,256]{6,5,4,3,2,0,1:T(8,128)(2,1)}, bf16[1,8,1,8,8,32,256]{6,5,4,3,2,0,1:T(8,128)(2,1)S(1)}, u32[]{:S(2)}) copy-start(bf16[1,8,1,8,8,32,256]{6,5,4,3,2,0,1:T(8,128)(2,1)S(1)} %get-tuple-element.18) | copy-start | bytes 25165828
  835.2 16.0 copy-start.1
  962.6 11.0 copy-start.2
  988.0 20.0 %copy-start.5 = (f32[4,2,8,8,32]{3,0,4,1,2:T(4,128)S(1)}, f32[4,2,8,8,32]{3,0,4,1,2:T(4,128)}, u32[]{:S(2)}) copy-start(f32[4,2,8,8,32]{3,0,4,1,2:T(4,128)} %copy.94) | copy-start | bytes 196612
  988.0 20.0 %copy-start.6 = (f32[4,2,8,8,32]{3,0,4,1,2:T(4,128)S(1)}, f32[4,2,8,8,32]{3,0,4,1,2:T(4,128)}, u32[]{:S(2)}) copy-start(f32[4,2,8,8,32]{3,0,4,1,2:T(4,128)} %copy.97) | copy-start | bytes 196612
  1592.3 15.1 slice-start
  1599.1 8.2 slice-start.1
  1599.1 8.2 copy-start.9
where the time goes:
time: 1630 us
  blocking collectives  465 us (29%)
  waiting for transfers between devices  451 us (28%)
  matrix products  364 us (22%)
  local copies, waits for them, and re-layouts  283 us (17%)
  other arithmetic  50.3 us (3%)
    all_to_all x1, blocking collectives, local(): lax.all_to_all(shaped, ('ba', 'col'), split_axis=2, concat_axis=1, tiled=...  368 us
    all_to_all x1, waiting for transfers between devices, local(): lax.all_to_all(shaped, ('ba', 'col'), split_axis=1, concat_axis=2, tiled=...  358 us
    dot_general x20, matrix products, contract(): return jnp.einsum(form, table, operand, preferred_element_type=jnp.float32)  314 us
    all_to_all x1, blocking collectives, local(): lax.all_to_all(conv_part, 'aa', split_axis=0, concat_axis=3, tiled=True)  97.2 us
    unnamed x27, local copies, waits for them, and re-layouts  95.7 us
    all_to_all x1, waiting for transfers between devices, local(): lax.all_to_all(local_block, 'aa', split_axis=3, concat_axis=0, tiled=True)  92.4 us
    all_to_all x1, local copies, waits for them, and re-layouts, local(): lax.all_to_all(local_block, 'aa', split_axis=3, concat_axis=0, tiled=True)  45.4 us
    reshape x1, local copies, waits for them, and re-layouts, local(): local_block = mixed.reshape(rows_i, rows_j, rows_k, D)  44.2 us
  transfers between devices with their start and end apart: 2, of which 2 were waited for; matrix products, arithmetic and copies ran while one was open for 0% of the time, Pallas kernels for 0%

commit v1 on v0

--- a/solution.py
+++ b/solution.py
@@ -32,6 +32,13 @@
 
 def contract(form, table, operand):
     return jnp.einsum(form, table, operand, preferred_element_type=jnp.float32)
+
+
+CHUNKS = 2
+
+
+def project(normed, weight):
+    return jnp.einsum("td,dgc->gtc", normed, weight, preferred_element_type=jnp.float32)
 
 
 def local(tokens, norm_gain, in_weight, skip_gain, spectrum_filter, out_weight):
@@ -48,11 +55,70 @@
     flat = tokens.reshape(-1, D).astype(jnp.float32)
     meansq = jnp.mean(flat * flat, axis=-1, keepdims=True)
     normed = (flat * lax.rsqrt(meansq + EPSILON) * norm_gain).astype(jnp.bfloat16)
-    projected = jnp.dot(normed, in_weight, preferred_element_type=jnp.float32)
-    mixed = (projected[:, :D] * projected[:, 2 * D :]).astype(jnp.bfloat16)
-    gate = projected[:, D : 2 * D].astype(jnp.bfloat16)
-    local_block = mixed.reshape(rows_i, rows_j, rows_k, D)
-    by_rows = lax.all_to_all(local_block, "aa", split_axis=3, concat_axis=0, tiled=True)
+    width = channels // CHUNKS
+    weights = in_weight.reshape(D, 3, count_aa, CHUNKS, width)
+    mixed = []
+    gate = []
+    for q in range(CHUNKS):
+        x1 = project(normed, weights[:, 0, :, q])
+        v = project(normed, weights[:, 2, :, q])
+        mixed.append((x1 * v).astype(jnp.bfloat16))
+    arrived = [
+        lax.all_to_all(part, "aa", split_axis=0, concat_axis=0, tiled=True) for part in mixed
+    ]
+    for q in range(CHUNKS):
+        gate.append(project(normed, weights[:, 1, :, q]).astype(jnp.bfloat16))
+    stages = [
+        spectral(
+            arrived[q].reshape(LA, rows_j, rows_k, width),
+            spectrum_filter[..., q * width : (q + 1) * width],
+        )
+        for q in range(CHUNKS)
+    ]
+    first = [None] * CHUNKS
+    moved = [None] * CHUNKS
+    back = [None] * CHUNKS
+    convs = [None] * CHUNKS
+    for q in range(CHUNKS):
+        first[q] = next(stages[q])
+        if q + 1 < CHUNKS:
+            first[q], arrived[q + 1] = lax.optimization_barrier((first[q], arrived[q + 1]))
+            stages[q + 1] = spectral(
+                arrived[q + 1].reshape(LA, rows_j, rows_k, width),
+                spectrum_filter[..., (q + 1) * width : (q + 2) * width],
+            )
+        moved[q] = stages[q].send(first[q])
+    for q in range(CHUNKS):
+        back[q] = stages[q].send(moved[q])
+        if q + 1 < CHUNKS:
+            back[q], moved[q + 1] = lax.optimization_barrier((back[q], moved[q + 1]))
+        convs[q] = stages[q].send(back[q])
+    gated = []
+    skips = skip_gain.reshape(count_aa, 1, CHUNKS, width)
+    for q in range(CHUNKS):
+        conv_part = convs[q]
+        conv_part = conv_part.reshape(count_aa, rows_i * rows_j * rows_k, width)
+        conv = lax.all_to_all(conv_part, "aa", split_axis=0, concat_axis=0, tiled=True)
+        conv = conv.astype(jnp.float32)
+        total = conv + skips[:, :, q] * mixed[q].astype(jnp.float32)
+        gated.append((gate[q].astype(jnp.float32) * total).astype(jnp.bfloat16))
+    joined = jnp.concatenate(gated, axis=-1)
+    out_blocks = out_weight.reshape(count_aa, channels, D)
+    layer_out = jnp.einsum(
+        "gtc,gcd->td", joined, out_blocks, preferred_element_type=jnp.float32
+    ).astype(jnp.bfloat16)
+    return layer_out.reshape(rows_i, rows_j, rows_k, D)
+
+
+def spectral(by_rows, spectrum_filter):
+    count_ba = lax.axis_size("ba")
+    count_col = lax.axis_size("col")
+    rows_j = LB // count_ba
+    rows_k = LC // count_col
+    blocks = count_ba * count_col
+    freq_local = LA // blocks
+    channels = by_rows.shape[-1]
+    points = LA * LB * LC
     cos_a, sin_a = dft_tables(LA)
     real_part = contract("fi,ijkx->fjkx", cos_a, by_rows)
     imag_part = -contract("fi,ijkx->fjkx", sin_a, by_rows)
@@ -67,8 +133,10 @@
     first = jnp.stack(
         [real_part * cos_phi + imag_part * sin_phi, imag_part * cos_phi - real_part * sin_phi]
     ).astype(jnp.bfloat16)
+    first = yield first
     shaped = first.reshape(2, blocks, 1, freq_local, rows_j, rows_k, channels)
     moved = lax.all_to_all(shaped, ("ba", "col"), split_axis=1, concat_axis=2, tiled=True)
+    moved = yield moved
     moved = moved.reshape(2, count_ba, count_col, freq_local, rows_j, rows_k, channels)
     cos_b, sin_b = dft_tables(LB)
     cos_b = cos_b.reshape(LB, count_ba, rows_j)
@@ -124,6 +192,7 @@
     back_second = jnp.stack(
         [real_part * cos_back - imag_part * sin_back, imag_part * cos_back + real_part * sin_back]
     ).astype(jnp.bfloat16)
+    back_second = yield back_second
     shaped = back_second.reshape(2, 1, blocks, freq_local, rows_j, rows_k, channels)
     returned = lax.all_to_all(shaped, ("ba", "col"), split_axis=2, concat_axis=1, tiled=True)
     returned = returned.reshape(2, LA, rows_j, rows_k, channels)
@@ -131,13 +200,7 @@
         contract("fi,fjkx->ijkx", cos_a, returned[0])
         - contract("fi,fjkx->ijkx", sin_a, returned[1])
     ).astype(jnp.bfloat16)
-    conv_tokens = lax.all_to_all(conv_part, "aa", split_axis=0, concat_axis=3, tiled=True)
-    conv_flat = conv_tokens.reshape(-1, D).astype(jnp.float32)
-    gated = (gate.astype(jnp.float32) * (conv_flat + skip_gain * mixed.astype(jnp.float32))).astype(
-        jnp.bfloat16
-    )
-    layer_out = jnp.dot(gated, out_weight, preferred_element_type=jnp.float32).astype(jnp.bfloat16)
-    return layer_out.reshape(rows_i, rows_j, rows_k, D)
+    yield conv_part
 
 
 def solution(mesh):

time: 1630 us -> 1080 us (0.66)
  blocking collectives: 465 us -> 0 us
  local copies, waits for them, and re-layouts: 283 us -> 142 us
  starting transfers between devices: 12.7 us -> 43 us
  waiting for transfers between devices: 451 us -> 476 us
  matrix products: 364 us -> 346 us
    all_to_all x2 -> x0, blocking collectives: 465 us -> none  [the longest x1 368 us: local(): lax.all_to_all(shaped, ('ba', 'col'), split_axis=2, concat_axis=1, tiled=...]
    unnamed x27 -> x61, local copies, waits for them, and re-layouts: 95.7 us -> 10.2 us
    unnamed x0 -> x6, matrix products: none -> 55.5 us
    dot_general x2 -> x1, matrix products: 50.1 us -> 11.6 us  [local(): jnp.einsum('gtc,gcd->td', joined, out_blocks, preferred_element_type=jnp....]
    dot_general x20 -> x40, matrix products: 314 us -> 279 us  [contract(): return jnp.einsum(form, table, operand, preferred_element_type=jnp.float32)]
    another operation x5, local copies, waits for them, and re-layouts: 61.2 us -> 27 us  [the longest x1 9.83 us: spectral(): jnp.stack([real_part * cos_back - imag_part * sin_back, imag_part * cos_b...]
    all_to_all x2 -> x8, starting transfers between devices: 12.7 us -> 43 us  [the longest x2 12.1 us: spectral(): lax.all_to_all(shaped, ('ba', 'col'), split_axis=1, concat_axis=2, tiled=...]
    all_to_all x1 -> x2, local copies, waits for them, and re-layouts: 45.4 us -> 16.2 us  [the longest x1 9.83 us: spectral(): lax.all_to_all(shaped, ('ba', 'col'), split_axis=1, concat_axis=2, tiled=...]
  transfers between devices with their start and end apart: 2 -> 8, of which waited for: 2 -> 8; matrix products, arithmetic and copies ran while one was open for 0% -> 42% of each run, Pallas kernels for 0% -> 0%
where the time goes in v1:
time: 1080 us; the launch traced here: 1070 us
  waiting for transfers between devices  476 us (44%)
  matrix products  346 us (32%)
  local copies, waits for them, and re-layouts  142 us (13%)
  other arithmetic  62.2 us (6%)
  starting transfers between devices  43 us (4%)
    dot_general x40, matrix products, contract(): return jnp.einsum(form, table, operand, preferred_element_type=jnp.float32)  279 us
    all_to_all x2, waiting for transfers between devices, spectral(): lax.all_to_all(shaped, ('ba', 'col'), split_axis=1, concat_axis=2, tiled=...  197 us
    all_to_all x2, waiting for transfers between devices, spectral(): lax.all_to_all(shaped, ('ba', 'col'), split_axis=2, concat_axis=1, tiled=...  192 us
    unnamed x6, matrix products  55.5 us
    all_to_all x2, waiting for transfers between devices, local(): lax.all_to_all(conv_part, 'aa', split_axis=0, concat_axis=0, tiled=True)  47.3 us
    all_to_all x2, waiting for transfers between devices, local(): lax.all_to_all(part, 'aa', split_axis=0, concat_axis=0, tiled=True)  39.1 us
  transfers between devices with their start and end apart: 8, of which 8 were waited for; matrix products, arithmetic and copies ran while one was open for 42% of the time, Pallas kernels for 0%

profile of v1, /device:TPU:0, one launch (start us, length us, event | category | flops | bytes accessed | tf_op | source)
XLA Modules:
  0.0 1070.2 jit_solution(11237887449495344365)
XLA Ops:
  0.0 8.8 copy.149
  19.1 6.8 fusion.453
  25.9 6.8 fusion.454
  32.7 9.0 fusion.32
  46.8 11.5 %fusion.455 = f32[4096,512]{0,1} fusion(bf16[4096,1024]{1,0:T(8,128)(2,1)} %bitcast.520, bf16[1024,512]{0,1:T(8,128)(2,1)} %bitcast.533), kind=kOutput, calls=%fused_computation.481 | convolution fusion | flops 4294967296 | bytes 17825792
  58.3 10.1 fusion.456
  68.4 9.0 fusion.35
  77.3 18.3 %all-to-all-done = bf16[4,4096,128]{1,2,0:T(8,128)(2,1)} async-done(((bf16[4,4096,128]{1,2,0:T(8,128)(2,1)}), bf16[4,4096,128]{1,2,0:T(8,128)(2,1)}, u32[]{:S(2)}, u32[]{:S(2)}) %all-to-all-start) | async-done | bytes 4194336 | tf_op jit(solution)/shard_map/all_to_all | solution.py:67
  101.6 6.4 copy.153
  113.7 8.3 fusion.33
  122.0 6.3 pad_maximum_fusion
  128.3 20.8 %all-to-all-done.1 = bf16[4,4096,128]{1,2,0:T(8,128)(2,1)} async-done(((bf16[4,4096,128]{1,2,0:T(8,128)(2,1)}), bf16[4,4096,128]{1,2,0:T(8,128)(2,1)}, u32[]{:S(2)}, u32[]{:S(2)}) %all-to-all-start.1) | async-done | bytes 4194336 | tf_op jit(solution)/shard_map/all_to_all | solution.py:67
  149.1 12.1 %copy.160 = bf16[2,8,1,8,8,32,128]{6,5,4,3,2,0,1:T(8,128)(2,1)} copy(bf16[2,8,1,8,8,32,128]{6,3,1,5,4,0,2:T(8,128)(2,1)} %bitcast.511) | data formatting | bytes 16777216 | tf_op jit(solution)/shard_map/reshape | solution.py:137
  161.2 6.9 all-to-all-start.2
  170.1 6.4 copy.179
  182.3 7.3 fusion.38
  197.1 6.3 pad_maximum_fusion.2
  203.3 147.5 %all-to-all-done.2 = bf16[2,8,1,8,8,32,128]{6,5,4,3,2,0,1:T(8,128)(2,1)} async-done(((bf16[2,8,1,8,8,32,128]{6,5,4,3,2,0,1:T(8,128)(2,1)}), bf16[2,8,1,8,8,32,128]{6,5,4,3,2,0,1:T(8,128)(2,1)}, u32[]{:S(2)}, u32[]{:S(2)}) %all-to-all-start.2) | async-done | bytes 8388640 | tf_op jit(solution)/shard_map/all_to_all | solution.py:138
  378.2 14.7 %fusion.28 = (bf16[8,32,2,32,128]{4,1,3,0,2:T(8,128)(2,1)}, bf16[8,32,2,32,128]{4,1,3,0,2:T(8,128)(2,1)S(1)}) fusion(f32[32,2,32]{0,2,1:T(8,128)S(1)} %get-tuple-element.54, f32[32,2,32]{0,2,1:T(8,128)S(1)} %get-tuple-element.53, f32[2,8,32,128,32,1]{3,4,5,2,1,0:T(8,128)} %fusion.110, f32[2,8,32,128,32,1]{3,4,5,2,1,0:T(8,128)} %fusion.108, ...), kind=kOutput, calls=%fused_computation.64 | convolution fusion | flops 155205632 | bytes 37765248 | tf_op jit(solution)/shard_map/gbj,bcfjkx->fgckx/dot_general | solution.py:34
  408.1 18.1 %fusion.47 = (bf16[8,32,64,128,1]{3,2,4,1,0:T(8,128)(2,1)}, bf16[8,32,64,128,1]{3,2,4,1,0:T(8,128)(2,1)}) fusion(f32[8,32,128,64,1]{2,3,4,1,0:T(8,128)} %fusion.98, f32[8,32,128,64,1]{2,3,4,1,0:T(8,128)} %fusion.100, f32[8,32,128,64,1]{2,3,4,1,0:T(8,128)} %fusion.96, bf16[2,8,32,64,256]{4,3,2,1,0:T(8,128)(2,1)} %param.10, ...), kind=kOutput, calls=%fused_computation.101 | convolution fusion | flops 293666816 | bytes 46137600 | tf_op jit(solution)/shard_map/hck,fgckx->fghx/dot_general | solution.py:34
  426.1 7.1 fusion.171
  442.6 12.6 %fusion.36 = (bf16[8,32,2,32,128,1]{4,3,2,1,0,5:T(8,128)(2,1)}, bf16[8,32,2,32,128,1]{4,3,2,1,0,5:T(8,128)(2,1)S(1)}) fusion(f32[32,2,32]{2,1,0:T(2,128)S(1)} %copy.172, f32[32,2,32]{2,1,0:T(2,128)S(1)} %copy.171, f32[8,32,128,2,32]{2,4,3,1,0:T(8,128)} %fusion.181, f32[8,32,128,2,32]{2,4,3,1,0:T(8,128)} %fusion.169, f32[8,32,128,2,32]{2,4,3,1,0:T(8,128)} %fusion.171, ...), kind=kOutput, calls=%fused_computation.90 | convolution fusion | flops 289472512 | bytes 37765376 | tf_op jit(solution)/shard_map/hck,fghx->fgckx/dot_general | solution.py:34
  457.9 6.0 fusion.68
  469.9 12.2 %fusion.43 = (bf16[1,4,2,8,8,32,128]{6,4,1,5,2,3,0:T(8,128)(2,1)S(1)}, bf16[1,4,2,8,8,32,128]{6,4,1,5,2,3,0:T(8,128)(2,1)}) fusion(f32[4,2,8,8,32]{3,0,4,1,2:T(4,128)} %copy.178, f32[4,2,8,8,32]{3,0,4,1,2:T(4,128)S(1)} %copy-done.25, f32[8,2,32,128,4,8]{3,5,4,2,1,0:T(8,128)S(1)} %copy-done.16, f32[8,2,32,128,4,8]{3,5,4,2,1,0:T(8,128)} %fusion.72, ...), kind=kOutput, calls=%fused_computation.97 | convolution fusion | flops 155205632 | bytes 37879936 | tf_op jit(solution)/shard_map/gbj,fgckx->bcfjkx/dot_general | solution.py:34
  482.1 6.2 pad_maximum_fusion.1
  488.3 49.8 %all-to-all-done.3 = bf16[2,8,1,8,8,32,128]{6,5,4,3,0,2,1:T(8,128)(2,1)} async-done(((bf16[2,8,1,8,8,32,128]{6,5,4,3,0,2,1:T(8,128)(2,1)}), bf16[2,8,1,8,8,32,128]{6,5,4,3,0,2,1:T(8,128)(2,1)}, u32[]{:S(2)}, u32[]{:S(2)}) %all-to-all-start.3) | async-done | bytes 8388640 | tf_op jit(solution)/shard_map/all_to_all | solution.py:138
  538.1 9.8 copy.376
  547.9 12.1 %copy.187 = bf16[2,4,2,8,8,32,128]{6,5,4,3,2,1,0:T(8,128)(2,1)} copy(bf16[2,4,2,8,8,32,128]{6,4,1,5,2,3,0:T(8,128)(2,1)} %pad_maximum_fusion.1) | data formatting | bytes 16777216 | tf_op jit(solution)/shard_map/optimization_barrier | solution.py:94
  560.0 9.8 copy.188
  594.3 14.5 %fusion.19 = (bf16[8,32,2,32,128]{4,1,3,0,2:T(8,128)(2,1)}, bf16[8,32,2,32,128]{4,1,3,0,2:T(8,128)(2,1)S(1)}) fusion(f32[32,2,32]{0,2,1:T(8,128)S(1)} %get-tuple-element.54, f32[32,2,32]{0,2,1:T(8,128)S(1)} %get-tuple-element.53, f32[2,8,32,128,32,1]{3,4,5,2,1,0:T(8,128)} %fusion.90, f32[2,8,32,128,32,1]{3,4,5,2,1,0:T(8,128)} %fusion.88, ...), kind=kOutput, calls=%fused_computation.42 | convolution fusion | flops 155205632 | bytes 37765248 | tf_op jit(solution)/shard_map/gbj,bcfjkx->fgckx/dot_general | solution.py:34
  624.0 18.1 %fusion.45 = (bf16[8,32,64,128,1]{3,2,4,1,0:T(8,128)(2,1)}, bf16[8,32,64,128,1]{3,2,4,1,0:T(8,128)(2,1)}) fusion(f32[8,32,128,64,1]{2,3,4,1,0:T(8,128)} %fusion.78, f32[8,32,128,64,1]{2,3,4,1,0:T(8,128)} %fusion.80, f32[8,32,128,64,1]{2,3,4,1,0:T(8,128)} %fusion.76, bf16[2,8,32,64,256]{4,3,2,1,0:T(8,128)(2,1)} %param.10, ...), kind=kOutput, calls=%fused_computation.99 | convolution fusion | flops 293666816 | bytes 46137600 | tf_op jit(solution)/shard_map/hck,fgckx->fghx/dot_general | solution.py:34
  642.0 7.1 fusion.165
  658.4 12.6 %fusion.40 = (bf16[8,32,2,32,128,1]{4,3,2,1,0,5:T(8,128)(2,1)S(1)}, bf16[8,32,2,32,128,1]{4,3,2,1,0,5:T(8,128)(2,1)}) fusion(f32[32,2,32]{2,1,0:T(2,128)S(1)} %copy.172, f32[32,2,32]{2,1,0:T(2,128)S(1)} %copy.171, f32[8,32,128,2,32]{2,4,3,1,0:T(8,128)} %fusion.175, f32[8,32,128,2,32]{2,4,3,1,0:T(8,128)} %fusion.163, f32[8,32,128,2,32]{2,4,3,1,0:T(8,128)} %fusion.165, ...), kind=kOutput, calls=%fused_computation.94 | convolution fusion | flops 289472512 | bytes 37765376 | tf_op jit(solution)/shard_map/hck,fghx->fgckx/dot_general | solution.py:34
  673.8 6.0 fusion.64
  679.8 6.0 fusion.62
  685.8 12.8 %fusion.15 = (bf16[4,2,8,8,32,128]{5,3,0,4,1,2:T(8,128)(2,1)}, bf16[4,2,8,8,32,128]{5,3,0,4,1,2:T(8,128)(2,1)}) fusion(f32[4,2,8,8,32]{3,0,4,1,2:T(4,128)S(1)} %copy-done.27, f32[4,2,8,8,32]{3,0,4,1,2:T(4,128)S(1)} %copy-done.26, f32[8,2,32,128,4,8]{3,5,4,2,1,0:T(8,128)S(1)} %copy-done.15, f32[8,2,32,128,4,8]{3,5,4,2,1,0:T(8,128)S(1)} %fusion.66, ...), kind=kOutput, calls=%fused_computation.32 | convolution fusion | flops 155205632 | bytes 37879936 | tf_op jit(solution)/shard_map/gbj,fgckx->bcfjkx/dot_general | solution.py:34
  708.4 6.2 pad_maximum_fusion.3
  714.6 9.8 copy.208
  724.5 32.9 %all-to-all-done.4 = bf16[2,1,8,8,8,32,128]{6,5,4,3,0,1,2:T(8,128)(2,1)} async-done(((bf16[2,1,8,8,8,32,128]{6,5,4,3,0,1,2:T(8,128)(2,1)}), bf16[2,1,8,8,8,32,128]{6,5,4,3,0,1,2:T(8,128)(2,1)}, u32[]{:S(2)}, u32[]{:S(2)}) %all-to-all-start.4) | async-done | bytes 8388640 | tf_op jit(solution)/shard_map/all_to_all | solution.py:197
  778.9 6.5 copy.192
  785.4 159.3 %all-to-all-done.6 = bf16[2,1,8,8,8,32,128]{6,5,4,3,1,0,2:T(8,128)(2,1)} async-done(((bf16[2,1,8,8,8,32,128]{6,5,4,3,1,0,2:T(8,128)(2,1)}), bf16[2,1,8,8,8,32,128]{6,5,4,3,1,0,2:T(8,128)(2,1)}, u32[]{:S(2)}, u32[]{:S(2)}) %all-to-all-start.6) | async-done | bytes 8388640 | tf_op jit(solution)/shard_map/all_to_all | solution.py:197
  949.8 10.2 fusion.452
  976.5 6.8 copy.212
  983.3 14.7 %all-to-all-done.5 = bf16[4,4096,128]{1,2,0:T(8,128)(2,1)} async-done(((bf16[4,4096,128]{1,2,0:T(8,128)(2,1)}), bf16[4,4096,128]{1,2,0:T(8,128)(2,1)}, u32[]{:S(2)}, u32[]{:S(2)}) %all-to-all-start.5) | async-done | bytes 4194336 | tf_op jit(solution)/shard_map/all_to_all | solution.py:101
  1002.9 10.2 fusion.457
  1018.5 32.6 %all-to-all-done.7 = bf16[4,4096,128]{1,2,0:T(8,128)(2,1)} async-done(((bf16[4,4096,128]{1,2,0:T(8,128)(2,1)}), bf16[4,4096,128]{1,2,0:T(8,128)(2,1)}, u32[]{:S(2)}, u32[]{:S(2)}) %all-to-all-start.7) | async-done | bytes 4194336 | tf_op jit(solution)/shard_map/all_to_all | solution.py:101
  1051.1 7.1 fusion.22
  1058.2 11.6 %bitcast_convert_fusion = bf16[4096,1024]{1,0:T(8,128)(2,1)} fusion(bf16[4,256,1024]{2,1,0:T(8,128)(2,1)S(1)} %bitcast.497, bf16[4,4096,128]{1,2,0:T(8,128)(2,1)S(1)} %fusion.22, bf16[4,4096,128]{1,2,0:T(8,128)(2,1)S(1)} %copy-done.20), kind=kOutput, calls=%fused_computation.5 | convolution fusion | flops 8610906112 | bytes 18874368 | tf_op jit(solution)/shard_map/gtc,gcd->td/dot_general | solution.py:107
  (123 shorter events, 217.6 us)
Async XLA Ops:
  0.0 1058.2 %copy-start = (bf16[1024,1024]{1,0:T(8,128)(2,1)S(1)}, bf16[1024,1024]{1,0:T(8,128)(2,1)}, u32[]{:S(2)}) copy-start(bf16[1024,1024]{1,0:T(8,128)(2,1)} %param.11) | copy-start | bytes 6291460
  8.8 6.4 copy-start.12
  8.8 8.1 copy-start.28
  19.1 6.8 copy-start.17
  41.7 53.9 %all-to-all-start = ((bf16[4,4096,128]{1,2,0:T(8,128)(2,1)}), bf16[4,4096,128]{1,2,0:T(8,128)(2,1)}, u32[]{:S(2)}, u32[]{:S(2)}) async-start(bf16[4,4096,128]{1,2,0:T(8,128)(2,1)} %fusion.32), calls=%async_computation | async-start | bytes 8388608 | tf_op jit(solution)/shard_map/all_to_all | solution.py:67
  95.6 53.4 %all-to-all-start.1 = ((bf16[4,4096,128]{1,2,0:T(8,128)(2,1)}), bf16[4,4096,128]{1,2,0:T(8,128)(2,1)}, u32[]{:S(2)}, u32[]{:S(2)}) async-start(bf16[4,4096,128]{1,2,0:T(8,128)(2,1)} %fusion.35), calls=%async_computation.1 | async-start | bytes 8388608 | tf_op jit(solution)/shard_map/all_to_all | solution.py:67
  108.0 5.7 copy-start.11
  161.2 189.7 %all-to-all-start.2 = ((bf16[2,8,1,8,8,32,128]{6,5,4,3,2,0,1:T(8,128)(2,1)}), bf16[2,8,1,8,8,32,128]{6,5,4,3,2,0,1:T(8,128)(2,1)}, u32[]{:S(2)}, u32[]{:S(2)}) async-start(bf16[2,8,1,8,8,32,128]{6,5,4,3,2,0,1:T(8,128)(2,1)} %copy.160), calls=%async_computation.2 | async-start | bytes 16777216 | tf_op jit(solution)/shard_map/all_to_all | solution.py:138
  176.5 5.7 copy-start.10
  203.3 153.1 %copy-start.24 = (f32[4,2,8,8,32]{4,3,2,1,0:T(8,128)S(1)}, f32[4,2,8,8,32]{4,3,2,1,0:T(8,128)}, u32[]{:S(2)}) copy-start(f32[4,2,8,8,32]{4,3,2,1,0:T(8,128)} %get-tuple-element.47) | copy-start | bytes 196612
  203.3 154.5 %copy-start.23 = (f32[4,2,8,8,32]{4,3,2,1,0:T(8,128)S(1)}, f32[4,2,8,8,32]{4,3,2,1,0:T(8,128)}, u32[]{:S(2)}) copy-start(f32[4,2,8,8,32]{4,3,2,1,0:T(8,128)} %get-tuple-element.48) | copy-start | bytes 196612
  350.9 187.2 %all-to-all-start.3 = ((bf16[2,8,1,8,8,32,128]{6,5,4,3,0,2,1:T(8,128)(2,1)}), bf16[2,8,1,8,8,32,128]{6,5,4,3,0,2,1:T(8,128)(2,1)}, u32[]{:S(2)}, u32[]{:S(2)}) async-start(bf16[2,8,1,8,8,32,128]{6,5,4,3,0,2,1:T(8,128)(2,1)} %pad_maximum_fusion.2), calls=%async_computation.3 | async-start | bytes 16777216 | tf_op jit(solution)/shard_map/all_to_all | solution.py:138
  363.4 9.9 copy-start.9
  398.0 5.1 copy-start.4
  426.1 7.1 copy-start.1
  433.2 4.7 copy-start.6
  457.8 6.0 copy-start.14
  463.9 6.0 copy-start.16
  463.9 6.0 copy-start.25
  569.8 187.5 %all-to-all-start.4 = ((bf16[2,1,8,8,8,32,128]{6,5,4,3,0,1,2:T(8,128)(2,1)}), bf16[2,1,8,8,8,32,128]{6,5,4,3,0,1,2:T(8,128)(2,1)}, u32[]{:S(2)}, u32[]{:S(2)}) async-start(bf16[2,1,8,8,8,32,128]{6,5,4,3,0,1,2:T(8,128)(2,1)} %copy.188), calls=%async_computation.4 | async-start | bytes 16777216 | tf_op jit(solution)/shard_map/all_to_all | solution.py:197
  579.5 9.9 copy-start.8
  613.9 5.1 copy-start.3
  642.0 7.1 copy-start.2
  649.1 4.7 copy-start.5
  673.8 6.0 copy-start.13
  679.7 6.0 copy-start.15
  679.7 6.0 copy-start.26
  679.7 6.0 copy-start.27
  698.7 5.1 copy-start.19
  757.3 187.4 %all-to-all-start.6 = ((bf16[2,1,8,8,8,32,128]{6,5,4,3,1,0,2:T(8,128)(2,1)}), bf16[2,1,8,8,8,32,128]{6,5,4,3,1,0,2:T(8,128)(2,1)}, u32[]{:S(2)}, u32[]{:S(2)}) async-start(bf16[2,1,8,8,8,32,128]{6,5,4,3,1,0,2:T(8,128)(2,1)} %copy.208), calls=%async_computation.6 | async-start | bytes 16777216 | tf_op jit(solution)/shard_map/all_to_all | solution.py:197
  778.9 170.9 %copy-start.22 = (bf16[1024,1,4,1,128]{0,4,3,2,1:T(8,128)(2,1)S(1)}, bf16[1024,1,4,1,128]{0,4,3,2,1:T(8,128)(2,1)}, u32[]{:S(2)}) copy-start(bf16[1024,1,4,1,128]{0,4,3,2,1:T(8,128)(2,1)} %get-tuple-element.41) | copy-start | bytes 3145732
  944.7 53.3 %all-to-all-start.5 = ((bf16[4,4096,128]{1,2,0:T(8,128)(2,1)}), bf16[4,4096,128]{1,2,0:T(8,128)(2,1)}, u32[]{:S(2)}, u32[]{:S(2)}) async-start(bf16[4,4096,128]{1,2,0:T(8,128)(2,1)} %copy.192), calls=%async_computation.5 | async-start | bytes 8388608 | tf_op jit(solution)/shard_map/all_to_all | solution.py:101
  976.5 26.4 %copy-start.29 = (f32[1024]{0:T(1024)S(1)}, f32[1024]{0:T(1024)}, u32[]{:S(2)}) copy-start(f32[1024]{0:T(1024)} %param.9) | copy-start | bytes 12292
  976.5 26.4 %copy-start.21 = (bf16[1024,1,4,1,128]{0,4,3,2,1:T(8,128)(2,1)S(1)}, bf16[1024,1,4,1,128]{0,4,3,2,1:T(8,128)(2,1)}, u32[]{:S(2)}) copy-start(bf16[1024,1,4,1,128]{0,4,3,2,1:T(8,128)(2,1)} %get-tuple-element.46) | copy-start | bytes 3145732
  998.0 53.1 %all-to-all-start.7 = ((bf16[4,4096,128]{1,2,0:T(8,128)(2,1)}), bf16[4,4096,128]{1,2,0:T(8,128)(2,1)}, u32[]{:S(2)}, u32[]{:S(2)}) async-start(bf16[4,4096,128]{1,2,0:T(8,128)(2,1)} %copy.212), calls=%async_computation.7 | async-start | bytes 8388608 | tf_op jit(solution)/shard_map/all_to_all | solution.py:101
  1002.9 10.3 copy-start.7
  1002.9 10.3 copy-start.18
  1051.1 7.2 copy-start.20
